TPU v7x, 32 devices: a whole 2x2x4 slice. The times are simulated.
32 devices in a mesh: row: 4 (over z), col: 8 (over y, x, core).
Axes of the slice: x: 2, y: 2, z: 4, core: 2. Of those that a mesh axis runs over, the one named last changes fastest.
Arguments:
- pair: bfloat16 [128, 128, 128], P('row', 'col'), may hold values from -6 to 6
- gain_in: float32 [128], replicated, may hold values from 0.1 to 1.9
- w_left_gate: bfloat16 [128, 128], replicated, may hold values from -0.5 to 0.5
- w_left: bfloat16 [128, 128], replicated, may hold values from -0.5 to 0.5
- w_right_gate: bfloat16 [128, 128], replicated, may hold values from -0.5 to 0.5
- w_right: bfloat16 [128, 128], replicated, may hold values from -0.5 to 0.5
- gain_out: float32 [128], replicated, may hold values from 0.1 to 1.9
- w_out_gate: bfloat16 [128, 128], replicated, may hold values from -0.5 to 0.5
- w_out: bfloat16 [128, 128], replicated, may hold values from -0.5 to 0.5
Outputs:
- update: bfloat16 [128, 128, 128], P('row', 'col')
All inputs are finite; a program needn't handle non-finite values.
Results may differ from a plain program's by a relative error of at most 0.0081.
Values may be sent and summed in bfloat16 or wider, within the bound.
A program may use at most 64 MiB of HBM per device.

v0:
```python
import jax
import jax.numpy as jnp
from jax import lax
from jax.sharding import PartitionSpec as P


def spread(value, axis, source):
    kept = jnp.where(lax.axis_index(axis) == source, value, 0).astype(value.dtype)
    return lax.psum(kept, axis)


def layer_norm(values, gain):
    mean = jnp.mean(values, axis=-1, keepdims=True)
    centred = values - mean
    variance = jnp.mean(centred * centred, axis=-1, keepdims=True)
    return centred * lax.rsqrt(variance + 1e-05) * gain


def project(normed, weight):
    return jnp.einsum("ijc,ch->ijh", normed, weight, preferred_element_type=jnp.float32)


def per_device(
    pair, gain_in, w_left_gate, w_left, w_right_gate, w_right, gain_out, w_out_gate, w_out
):
    col_block = pair.shape[1]
    normed = layer_norm(pair.astype(jnp.float32), gain_in).astype(jnp.bfloat16)
    left = (jax.nn.sigmoid(project(normed, w_left_gate)) * project(normed, w_left)).astype(
        jnp.bfloat16
    )
    right = (jax.nn.sigmoid(project(normed, w_right_gate)) * project(normed, w_right)).astype(
        jnp.bfloat16
    )
    panel = lax.all_gather(right, "col", axis=1, tiled=True)
    ratio = lax.axis_size("col") // lax.axis_size("row")
    column = lax.axis_index("col")
    owned = lax.dynamic_slice_in_dim(panel, column % ratio * col_block, col_block, 0)
    right_cols = spread(owned, "row", column // ratio)
    mixed = jnp.einsum(
        "ikh,jkh->ijh",
        lax.all_gather(left, "col", axis=1, tiled=True),
        right_cols,
        preferred_element_type=jnp.float32,
    )
    out_normed = layer_norm(mixed, gain_out).astype(jnp.bfloat16)
    gate = jax.nn.sigmoid(project(normed, w_out_gate))
    return (gate * project(out_normed, w_out)).astype(jnp.bfloat16)


def solution(mesh):
    return jax.shard_map(
        per_device,
        mesh=mesh,
        in_specs=(P("row", "col", None), P(), P(), P(), P(), P(), P(), P(), P()),
        out_specs=P("row", "col", None),
        check_vma=False,
    )
```

profile of v0, /device:TPU:0, one launch (start us, length us, event | category | flops | bytes accessed | tf_op | source)
XLA Modules:
  0.0 118.3 jit_solution(17860925446135129522)
XLA Ops:
  6.5 0.0 copy-start
  6.5 0.0 copy-start.1
  6.5 0.0 copy-start.3
  6.5 0.0 copy-start.5
  6.5 0.0 all-gather.3.cloned.1.call-start
  6.6 1.1 convert_reduce_fusion
  7.7 0.1 copy.27
  7.8 0.1 copy.28
  7.8 1.1 fusion.14
  9.0 0.1 copy.29
  9.1 0.1 copy.30
  9.2 0.0 copy-done
  9.2 1.2 %fusion.5 = f32[32,16,128]{2,1,0:T(8,128)S(1)} fusion(bf16[128,128]{1,0:T(8,128)(2,1)S(1)} %copy-done, bf16[32,16,128]{2,1,0:T(8,128)(2,1)} %param.9, f32[128]{0:T(128)} %param.10, f32[32,16]{1,0:T(8,128)S(1)} %copy.30, f32[32,16]{1,0:T(8,128)S(1)} %copy.28), kind=kOutput, calls=%fused_computation.11 | convolution fusion | flops 17301504 | bytes 430592 | tf_op jit(solution)/shard_map/ijc,ch->ijh/dot_general | solution.py:20
  10.4 1.9 %fusion.9 = bf16[32,16,128]{2,1,0:T(8,128)(2,1)} fusion(f32[32,16,128]{2,1,0:T(8,128)S(1)} %fusion.5, bf16[128,128]{1,0:T(8,128)(2,1)} %param.14, bf16[32,16,128]{2,1,0:T(8,128)(2,1)} %param.9, f32[128]{0:T(128)} %param.10, f32[32,16]{1,0:T(8,128)S(1)} %copy.30, f32[32,16]{1,0:T(8,128)S(1)} %copy.28), kind=kOutput, calls=%fused_computation.16 | convolution fusion | flops 17235968 | bytes 561664 | tf_op jit(solution)/shard_map/ijc,ch->ijh/dot_general | solution.py:20
  12.3 0.0 all-gather.3.cloned.1.call-update
  12.3 0.0 all-gather.5.cloned.1.call-start
  12.4 1.3 %fusion.2 = f32[32,16,128]{2,1,0:T(8,128)S(1)} fusion(bf16[128,128]{1,0:T(8,128)(2,1)} %param.11, bf16[32,16,128]{2,1,0:T(8,128)(2,1)} %param.9, f32[128]{0:T(128)} %param.10, f32[32,16]{1,0:T(8,128)S(1)} %copy.30, f32[32,16]{1,0:T(8,128)S(1)} %copy.28), kind=kOutput, calls=%fused_computation.7 | convolution fusion | flops 17301504 | bytes 430592 | tf_op jit(solution)/shard_map/ijc,ch->ijh/dot_general | solution.py:20
  13.7 1.9 %fusion.10 = bf16[32,16,128]{2,1,0:T(8,128)(2,1)} fusion(f32[32,16,128]{2,1,0:T(8,128)S(1)} %fusion.2, bf16[128,128]{1,0:T(8,128)(2,1)} %param.12, bf16[32,16,128]{2,1,0:T(8,128)(2,1)} %param.9, f32[128]{0:T(128)} %param.10, f32[32,16]{1,0:T(8,128)S(1)} %copy.30, f32[32,16]{1,0:T(8,128)S(1)} %copy.28), kind=kOutput, calls=%fused_computation.17 | convolution fusion | flops 17235968 | bytes 561664 | tf_op jit(solution)/shard_map/ijc,ch->ijh/dot_general | solution.py:20
  15.6 0.0 all-gather.5.cloned.1.call-update
  15.6 0.0 all-reduce.2.cloned.1.call-start
  15.7 23.1 %all-gather.3.cloned.1.call-done = bf16[32,128,128]{2,1,0:T(8,128)(2,1)} async-done(((bf16[32,16,128]{2,1,0:T(8,128)(2,1)}), bf16[32,128,128]{2,1,0:T(8,128)(2,1)}) %all-gather.3.cloned.1.call-update) | async-done | bytes 1048592 | tf_op jit(solution)/shard_map/all_gather | solution.py:34
  38.7 1.9 %dynamic-slice_select_fusion = bf16[16,128,128]{2,1,0:T(8,128)(2,1)} fusion(bf16[32,128,128]{2,1,0:T(8,128)(2,1)} %all-gather.3.cloned.1.call-done, s32[]{:T(128)S(6)} %select_n.25, pred[]{:T(512)S(6)} %eq.5), kind=kLoop, calls=%fused_computation.21 | loop fusion | flops 262144 | bytes 1048581 | tf_op jit(solution)/shard_map/jit(_where)/select_n | solution.py:8
  40.6 0.0 all-reduce.2.cloned.1.call-update
  40.6 0.0 copy-done.1
  40.6 0.0 copy-done.3
  40.6 0.0 copy-done.5
  40.6 0.3 fusion.8
  41.0 23.1 %all-gather.5.cloned.1.call-done = bf16[32,128,128]{2,1,0:T(8,128)(2,1)} async-done(((bf16[32,16,128]{2,1,0:T(8,128)(2,1)}), bf16[32,128,128]{2,1,0:T(8,128)(2,1)}) %all-gather.5.cloned.1.call-update) | async-done | bytes 1048592 | tf_op jit(solution)/shard_map/all_gather | solution.py:41
  64.1 8.6 %copy.32 = bf16[32,128,128]{0,1,2:T(8,128)(2,1)} copy(bf16[32,128,128]{2,1,0:T(8,128)(2,1)} %all-gather.5.cloned.1.call-done) | data formatting | bytes 2097152 | tf_op jit(solution)/shard_map/all_gather | solution.py:41
  72.7 0.0 copy-start.4
  72.7 32.4 %all-reduce.2.cloned.1.call-done = bf16[16,128,128]{2,1,0:T(8,128)(2,1)} async-done(((bf16[16,128,128]{2,1,0:T(8,128)(2,1)}), bf16[16,128,128]{2,1,0:T(8,128)(2,1)}) %all-reduce.2.cloned.1.call-update) | async-done | bytes 524304 | tf_op jit(solution)/shard_map/psum | solution.py:9
  105.1 1.5 %copy.31 = bf16[16,128,128]{1,0,2:T(8,128)(2,1)S(1)} copy(bf16[16,128,128]{2,1,0:T(8,128)(2,1)} %all-reduce.2.cloned.1.call-done) | data formatting | bytes 1048576 | tf_op jit(solution)/shard_map/psum | solution.py:9
  106.6 0.0 copy-start.2
  106.6 3.4 %fusion.28 = (f32[32,16]{0,1:T(8,128)S(1)}, f32[32,16,128]{0,1,2:T(8,128)S(1)}) fusion(bf16[16,128,128]{1,0,2:T(8,128)(2,1)S(1)} %copy.31, bf16[32,128,128]{0,1,2:T(8,128)(2,1)} %copy.32), kind=kOutput, calls=%fused_computation.39 | convolution fusion | flops 16842240 | bytes 1837056 | tf_op jit(solution)/shard_map/ikh,jkh->ijh/dot_general | solution.py:39
  110.0 0.2 multiply_reduce_fusion
  110.2 0.0 copy-done.4
  110.2 0.2 multiply_convert_fusion
  110.4 0.5 copy.33
  110.9 0.0 copy-done.2
  110.9 0.8 fusion.11
  (4 shorter events, 0.0 us)
Async XLA Ops:
  6.5 2.6 %copy-start = (bf16[128,128]{1,0:T(8,128)(2,1)S(1)}, bf16[128,128]{1,0:T(8,128)(2,1)}, u32[]{:S(2)}) copy-start(bf16[128,128]{1,0:T(8,128)(2,1)} %param.13) | copy-start | bytes 98308
  6.5 34.1 %copy-start.1 = (bf16[32,16,128]{2,1,0:T(8,128)(2,1)S(1)}, bf16[32,16,128]{2,1,0:T(8,128)(2,1)}, u32[]{:S(2)}) copy-start(bf16[32,16,128]{2,1,0:T(8,128)(2,1)} %param.9) | copy-start | bytes 393220
  6.5 34.1 %copy-start.3 = (f32[128]{0:T(128)S(1)}, f32[128]{0:T(128)}, u32[]{:S(2)}) copy-start(f32[128]{0:T(128)} %param.10) | copy-start | bytes 1540
  6.5 34.1 %copy-start.5 = (bf16[128,128]{1,0:T(8,128)(2,1)S(1)}, bf16[128,128]{1,0:T(8,128)(2,1)}, u32[]{:S(2)}) copy-start(bf16[128,128]{1,0:T(8,128)(2,1)} %param.16) | copy-start | bytes 98308
  6.5 32.2 %all-gather.3.cloned.1.call-start = ((), (), s32[]{:S(2)}) async-start(), calls=%async_computation | async-start | bytes 1179648 | tf_op jit(solution)/shard_map/all_gather | solution.py:34
  12.3 51.7 %all-gather.5.cloned.1.call-start = ((), (), s32[]{:S(2)}) async-start(), calls=%async_computation.2 | async-start | bytes 1179648 | tf_op jit(solution)/shard_map/all_gather | solution.py:41
  15.6 89.5 %all-reduce.2.cloned.1.call-start = ((), (), s32[]{:S(2)}) async-start(), calls=%async_computation.1 | async-start | bytes 1048576 | tf_op jit(solution)/shard_map/psum | solution.py:9
  72.7 37.5 %copy-start.4 = (f32[128]{0:T(128)S(1)}, f32[128]{0:T(128)}, u32[]{:S(2)}) copy-start(f32[128]{0:T(128)} %param.15) | copy-start | bytes 1540
  106.6 4.4 %copy-start.2 = (bf16[128,128]{1,0:T(8,128)(2,1)S(1)}, bf16[128,128]{1,0:T(8,128)(2,1)}, u32[]{:S(2)}) copy-start(bf16[128,128]{1,0:T(8,128)(2,1)} %param.17) | copy-start | bytes 98308
Sparse Core Ops, SparseCore 0:
  12.5 26.1 all-gather.2
  40.6 23.4 all-gather.4
  66.4 38.6 all-reduce.1
where the time goes:
time: 119 us; the launch traced here: 118 us
  waiting for transfers between devices  78.6 us (66%)
  between operations  13.3 us (11%)
  local copies, waits for them, and re-layouts  10.9 us (9%)
  matrix products  10.9 us (9%)
  other arithmetic  4.59 us (4%)
    psum x1, waiting for transfers between devices, spread(): return lax.psum(kept, axis)  32.4 us
    all_gather x1, waiting for transfers between devices, per_device(): lax.all_gather(left, 'col', axis=1, tiled=True)  23.1 us
    all_gather x1, waiting for transfers between devices, per_device(): panel = lax.all_gather(right, 'col', axis=1, tiled=True)  23.1 us
    all_gather x1, local copies, waits for them, and re-layouts, per_device(): lax.all_gather(left, 'col', axis=1, tiled=True)  8.61 us
    dot_general x6, matrix products, project(): jnp.einsum('ijc,ch->ijh', normed, weight, preferred_element_type=jnp.floa...  7.46 us
    dot_general x1, matrix products, per_device(): jnp.einsum('ikh,jkh->ijh', lax.all_gather(left, 'col', axis=1, tiled=True...  3.39 us
  transfers between devices with their start and end apart: 3, of which 3 were waited for; matrix products, arithmetic and copies ran while one was open for 12% of the time, Pallas kernels for 0%

commit v1 on v0

v1 whole, which is shorter than its diff:
```python
import functools

import jax
import jax.numpy as jnp
from jax import lax
from jax.experimental import pallas as pl
from jax.experimental.pallas import tpu as pltpu
from jax.sharding import PartitionSpec as P

MESH = pl.DeviceIdType.MESH
F32 = jnp.float32
BF16 = jnp.bfloat16
GROUP = 8


def layer_norm(values, gain):
    mean = jnp.mean(values, axis=-1, keepdims=True)
    centred = values - mean
    variance = jnp.mean(centred * centred, axis=-1, keepdims=True)
    return centred * lax.rsqrt(variance + 1e-05) * gain


def gated(normed, w_gate, w):
    gate = jnp.dot(normed, w_gate, preferred_element_type=F32)
    value = jnp.dot(normed, w, preferred_element_type=F32)
    return (jax.nn.sigmoid(gate) * value).astype(BF16)


def kernel(
    nr, nc,
    pair, gain_in, w_left_gate, w_left, w_right_gate, w_right, gain_out, w_out_gate, w_out,
    out,
    normed_f, normed_t, gate, left_buf, right_own, right_buf, left_f, acc,
    left_send, left_fwd, left_recv, right_send, right_recv,
):
    rows, cols, width = pair.shape
    ratio = nc // nr
    chips = nc // 2
    r = lax.axis_index("row")
    c = lax.axis_index("col")
    chip, core = c // 2, c % 2
    sibling = chip * 2 + 1 - core
    home = c // ratio

    def same_core(a):
        return (chip + a) % chips * 2 + core

    def other_core(a):
        return (chip + a) % chips * 2 + 1 - core

    barrier = pltpu.get_barrier_semaphore()
    def greet(row, col):
        pl.semaphore_signal(barrier, inc=1, device_id={"row": row, "col": col}, device_id_type=MESH)
    greet(r, sibling)
    for a in range(1, chips):
        greet(r, same_core(a))
    for s in range(1, nc):
        greet(home, (c + s) % nc)
    @pl.when(home != r)
    def _():
        greet(home, c)

    normed = layer_norm(pair[...].reshape(rows * cols, width).astype(F32), gain_in[...])
    normed_f[...] = normed
    normed = normed.astype(BF16)
    left_buf[c] = gated(normed, w_left_gate[...], w_left[...])
    for t in range(ratio):
        for k in range(cols):
            normed_t[pl.ds((t * cols + k) * cols, cols), :] = normed_f[
                pl.ds(t * cols * cols + k, cols, stride=cols), :
            ].astype(BF16)
    right = gated(normed_t[...], w_right_gate[...], w_right[...])
    right_own[...] = right.reshape(ratio, cols, cols, width)

    left_peers = chips
    total = left_peers + nr * ratio
    self_right = (home == r).astype(jnp.int32)
    pl.semaphore_wait(barrier, total - self_right)

    def left_copy(block, col, sem):
        return pltpu.make_async_remote_copy(
            src_ref=left_buf.at[block], dst_ref=left_buf.at[block],
            send_sem=sem, recv_sem=left_recv.at[block],
            device_id={"row": r, "col": col}, device_id_type=MESH,
        )

    def right_copy(dz, t):
        return pltpu.make_async_remote_copy(
            src_ref=right_own.at[t], dst_ref=right_buf.at[c],
            send_sem=right_send.at[dz * ratio + t], recv_sem=right_recv.at[c],
            device_id={"row": (r + dz) % nr, "col": r * ratio + t}, device_id_type=MESH,
        )

    def right_local(t):
        return pltpu.make_async_copy(right_own.at[t], right_buf.at[c], right_recv.at[c])

    for a in range(1, chips):
        left_copy(c, same_core(a), left_send.at[a]).start()
    left_copy(c, sibling, left_send.at[0]).start()
    for dz in list(range(1, nr)) + [0]:
        for t in range(ratio):
            if dz:
                right_copy(dz, t).start()
            else:
                here = r * ratio + t == c
                @pl.when(here)
                def _(t=t):
                    right_local(t).start()
                @pl.when(jnp.logical_not(here))
                def _(t=t):
                    right_copy(0, t).start()

    gate[...] = jax.nn.sigmoid(jnp.dot(normed, w_out_gate[...], preferred_element_type=F32))
    acc[...] = jnp.zeros_like(acc)

    for a in range(1, chips):
        block = same_core(a)
        left_copy(block, sibling, left_fwd.at[a]).wait_recv()
        left_copy(block, sibling, left_fwd.at[a]).start()

    def mix(block):
        pltpu.make_async_remote_copy(
            src_ref=right_own.at[0], dst_ref=right_buf.at[block],
            send_sem=right_send.at[0], recv_sem=right_recv.at[block],
            device_id={"row": r, "col": sibling}, device_id_type=MESH,
        ).wait_recv()
        left_f[...] = left_buf[block].astype(F32).reshape(rows, cols, width)

        def group(g, carry):
            sums = [acc[g * GROUP + n] for n in range(GROUP)]
            for k in range(cols):
                other = right_buf[block, k].astype(F32)
                for n in range(GROUP):
                    sums[n] = sums[n] + left_f[g * GROUP + n, pl.ds(k, 1), :] * other
            for n in range(GROUP):
                acc[g * GROUP + n] = sums[n]
            return carry

        lax.fori_loop(0, rows // GROUP, group, 0)

    def own_core(a, carry):
        mix(same_core(a))
        return carry

    def their_core(a, carry):
        block = other_core(a)
        left_copy(block, sibling, left_send.at[0]).wait_recv()
        mix(block)
        return carry

    lax.fori_loop(0, chips, own_core, 0)
    lax.fori_loop(0, chips, their_core, 0)

    mixed = acc[...].reshape(rows * cols, width)
    out_normed = layer_norm(mixed, gain_out[...]).astype(BF16)
    update = gate[...] * jnp.dot(out_normed, w_out[...], preferred_element_type=F32)
    out[...] = update.astype(BF16).reshape(rows, cols, width)

    left_copy(c, sibling, left_send.at[0]).wait_send()
    for a in range(1, chips):
        left_copy(c, same_core(a), left_send.at[a]).wait_send()
        left_copy(same_core(a), sibling, left_fwd.at[a]).wait_send()
    for dz in range(nr):
        for t in range(ratio):
            if dz:
                right_copy(dz, t).wait_send()
            else:
                @pl.when(r * ratio + t != c)
                def _(t=t):
                    right_copy(0, t).wait_send()


def solution(mesh):
    nr, nc = mesh.shape["row"], mesh.shape["col"]

    def per_device(
        pair, gain_in, w_left_gate, w_left, w_right_gate, w_right, gain_out, w_out_gate, w_out
    ):
        rows, cols, width = pair.shape
        flat = rows * cols
        ratio = nc // nr
        dma = pltpu.SemaphoreType.DMA
        return pl.pallas_call(
            functools.partial(kernel, nr, nc),
            out_shape=jax.ShapeDtypeStruct(pair.shape, BF16),
            in_specs=[pl.BlockSpec(memory_space=pltpu.VMEM)] * 9,
            out_specs=pl.BlockSpec(memory_space=pltpu.VMEM),
            scratch_shapes=[
                pltpu.VMEM((flat, width), F32),
                pltpu.VMEM((flat, width), BF16),
                pltpu.VMEM((flat, width), F32),
                pltpu.VMEM((nc, flat, width), BF16),
                pltpu.VMEM((ratio, cols, cols, width), BF16),
                pltpu.VMEM((nc, cols, cols, width), BF16),
                pltpu.VMEM((rows, cols, width), F32),
                pltpu.VMEM((rows, cols, width), F32),
                dma((nc // 2,)),
                dma((nc // 2,)),
                dma((nc,)),
                dma((nr * ratio,)),
                dma((nc,)),
            ],
            compiler_params=pltpu.CompilerParams(collective_id=0, has_side_effects=True),
        )(
            pair, gain_in.reshape(1, -1), w_left_gate, w_left, w_right_gate, w_right,
            gain_out.reshape(1, -1), w_out_gate, w_out,
        )

    return jax.shard_map(
        per_device,
        mesh=mesh,
        in_specs=(P("row", "col", None), P(), P(), P(), P(), P(), P(), P(), P()),
        out_specs=P("row", "col", None),
        check_vma=False,
    )
```

time: 119 us -> 26 us (0.22)
  the two profiles are of different devices: /device:TPU:0 before, /device:TPU:12 now
where the time goes in v1:
time: 26 us; the launch traced here: 25.9 us
  Pallas kernels  24.3 us (93%)
  local copies, waits for them, and re-layouts  1.57 us (6%)
    pallas_call x1, Pallas kernels, per_device(): pl.pallas_call(functools.partial(kernel, nr, nc), out_shape=jax.ShapeDtyp...  24.3 us
    unnamed x1, local copies, waits for them, and re-layouts  1.57 us

profile of v1, /device:TPU:12, one launch (start us, length us, event | category | flops | bytes accessed | tf_op | source)
XLA Modules:
  0.0 25.9 jit_solution(5479804389067487654)
XLA Ops:
  0.0 24.3 %shard_map.91 = bf16[32,16,128]{2,1,0:T(8,128)(2,1)} custom-call(bf16[32,16,128]{2,1,0:T(8,128)(2,1)} %pair.1, f32[1,128]{1,0:T(1,128)} %bitcast.2, bf16[128,128]{1,0:T(8,128)(2,1)} %w_left_gate.1, bf16[128,128]{1,0:T(8,128)(2,1)} %w_left.1, bf16[128,128]{1,0:T(8,128)(2,1)} %w_right_gate.1, bf16[128,128]{1,0:T(8,128)(2,1)} %w_right.1, f32[1,128]{1,0:T(1,128)} %bitcast.3, ...), custom_call_target="tpu_custom_call" | custom-call | tf_op jit(solution)/shard_map/pallas_call | solution.py:183
  24.3 1.6 %copy.11 = bf16[32,16,128]{2,1,0:T(8,128)(2,1)} copy(bf16[32,16,128]{2,1,0:T(8,128)(2,1)} %shard_map.91) | data formatting | bytes 262144

commit v2 on v1

--- a/solution.py
+++ b/solution.py
@@ -30,8 +30,8 @@
     nr, nc,
     pair, gain_in, w_left_gate, w_left, w_right_gate, w_right, gain_out, w_out_gate, w_out,
     out,
-    normed_f, normed_t, gate, left_buf, right_own, right_buf, left_f, acc,
-    left_send, left_fwd, left_recv, right_send, right_recv,
+    normed_f, normed_t, gate, left_buf, chain, right_buf, left_f, acc,
+    left_send, left_fwd, left_recv, right_send, right_recv, up_send, down_send, chain_recv,
 ):
     rows, cols, width = pair.shape
     ratio = nc // nr
@@ -40,7 +40,6 @@
     c = lax.axis_index("col")
     chip, core = c // 2, c % 2
     sibling = chip * 2 + 1 - core
-    home = c // ratio
 
     def same_core(a):
         return (chip + a) % chips * 2 + core
@@ -49,79 +48,123 @@
         return (chip + a) % chips * 2 + 1 - core
 
     barrier = pltpu.get_barrier_semaphore()
+
     def greet(row, col):
         pl.semaphore_signal(barrier, inc=1, device_id={"row": row, "col": col}, device_id_type=MESH)
-    greet(r, sibling)
-    for a in range(1, chips):
-        greet(r, same_core(a))
+
     for s in range(1, nc):
-        greet(home, (c + s) % nc)
-    @pl.when(home != r)
+        greet(r, (c + s) % nc)
+
+    @pl.when(r > 0)
     def _():
-        greet(home, c)
+        greet(r - 1, c)
+
+    @pl.when(r < nr - 1)
+    def _():
+        greet(r + 1, c)
+
+    def chain_copy(block, t, row, sem):
+        return pltpu.make_async_remote_copy(
+            src_ref=chain.at[block, t], dst_ref=chain.at[block, t],
+            send_sem=sem, recv_sem=chain_recv.at[block, t],
+            device_id={"row": row, "col": c}, device_id_type=MESH,
+        )
+
+    def right_copy(block, t):
+        return pltpu.make_async_remote_copy(
+            src_ref=chain.at[block, t], dst_ref=right_buf.at[c],
+            send_sem=right_send.at[block, t], recv_sem=right_recv.at[c],
+            device_id={"row": r, "col": block * ratio + t}, device_id_type=MESH,
+        )
+
+    def left_copy(block, col, sem):
+        return pltpu.make_async_remote_copy(
+            src_ref=left_buf.at[block], dst_ref=left_buf.at[block],
+            send_sem=sem, recv_sem=left_recv.at[block],
+            device_id={"row": r, "col": col}, device_id_type=MESH,
+        )
+
+    def deliver(block, t):
+        here = block * ratio + t == c
+
+        @pl.when(here)
+        def _():
+            pltpu.make_async_copy(chain.at[block, t], right_buf.at[c], right_recv.at[c]).start()
+
+        @pl.when(jnp.logical_not(here))
+        def _():
+            right_copy(block, t).start()
 
     normed = layer_norm(pair[...].reshape(rows * cols, width).astype(F32), gain_in[...])
     normed_f[...] = normed
-    normed = normed.astype(BF16)
-    left_buf[c] = gated(normed, w_left_gate[...], w_left[...])
     for t in range(ratio):
         for k in range(cols):
             normed_t[pl.ds((t * cols + k) * cols, cols), :] = normed_f[
                 pl.ds(t * cols * cols + k, cols, stride=cols), :
             ].astype(BF16)
     right = gated(normed_t[...], w_right_gate[...], w_right[...])
-    right_own[...] = right.reshape(ratio, cols, cols, width)
-
-    left_peers = chips
-    total = left_peers + nr * ratio
-    self_right = (home == r).astype(jnp.int32)
-    pl.semaphore_wait(barrier, total - self_right)
-
-    def left_copy(block, col, sem):
-        return pltpu.make_async_remote_copy(
-            src_ref=left_buf.at[block], dst_ref=left_buf.at[block],
-            send_sem=sem, recv_sem=left_recv.at[block],
-            device_id={"row": r, "col": col}, device_id_type=MESH,
-        )
-
-    def right_copy(dz, t):
-        return pltpu.make_async_remote_copy(
-            src_ref=right_own.at[t], dst_ref=right_buf.at[c],
-            send_sem=right_send.at[dz * ratio + t], recv_sem=right_recv.at[c],
-            device_id={"row": (r + dz) % nr, "col": r * ratio + t}, device_id_type=MESH,
-        )
-
-    def right_local(t):
-        return pltpu.make_async_copy(right_own.at[t], right_buf.at[c], right_recv.at[c])
-
+    chain[r] = right.reshape(ratio, cols, cols, width)
+
+    pl.semaphore_wait(
+        barrier, nc - 1 + (r > 0).astype(jnp.int32) + (r < nr - 1).astype(jnp.int32)
+    )
+
+    for t in range(ratio):
+        @pl.when(r < nr - 1)
+        def _(t=t):
+            chain_copy(r, t, r + 1, up_send.at[r, t]).start()
+
+        @pl.when(r > 0)
+        def _(t=t):
+            chain_copy(r, t, r - 1, down_send.at[r, t]).start()
+
+    normed = normed.astype(BF16)
+    left_buf[c] = gated(normed, w_left_gate[...], w_left[...])
+    for t in range(ratio):
+        deliver(r, t)
     for a in range(1, chips):
         left_copy(c, same_core(a), left_send.at[a]).start()
     left_copy(c, sibling, left_send.at[0]).start()
-    for dz in list(range(1, nr)) + [0]:
-        for t in range(ratio):
-            if dz:
-                right_copy(dz, t).start()
-            else:
-                here = r * ratio + t == c
-                @pl.when(here)
-                def _(t=t):
-                    right_local(t).start()
-                @pl.when(jnp.logical_not(here))
-                def _(t=t):
-                    right_copy(0, t).start()
 
     gate[...] = jax.nn.sigmoid(jnp.dot(normed, w_out_gate[...], preferred_element_type=F32))
     acc[...] = jnp.zeros_like(acc)
 
+    def relay(d):
+        for t in range(ratio):
+            @pl.when(r - d >= 0)
+            def _(t=t):
+                block = r - d
+                chain_copy(block, t, r, up_send.at[block, t]).wait_recv()
+
+                @pl.when(r < nr - 1)
+                def _():
+                    chain_copy(block, t, r + 1, up_send.at[block, t]).start()
+
+                deliver(block, t)
+
+            @pl.when(r + d < nr)
+            def _(t=t):
+                block = r + d
+                chain_copy(block, t, r, down_send.at[block, t]).wait_recv()
+
+                @pl.when(r > 0)
+                def _():
+                    chain_copy(block, t, r - 1, down_send.at[block, t]).start()
+
+                deliver(block, t)
+
+    for d in range(1, nr - 1):
+        relay(d)
     for a in range(1, chips):
         block = same_core(a)
         left_copy(block, sibling, left_fwd.at[a]).wait_recv()
         left_copy(block, sibling, left_fwd.at[a]).start()
+    relay(nr - 1)
 
     def mix(block):
         pltpu.make_async_remote_copy(
-            src_ref=right_own.at[0], dst_ref=right_buf.at[block],
-            send_sem=right_send.at[0], recv_sem=right_recv.at[block],
+            src_ref=chain.at[0, 0], dst_ref=right_buf.at[block],
+            send_sem=right_send.at[0, 0], recv_sem=right_recv.at[block],
             device_id={"row": r, "col": sibling}, device_id_type=MESH,
         ).wait_recv()
         left_f[...] = left_buf[block].astype(F32).reshape(rows, cols, width)
@@ -160,14 +203,19 @@
     for a in range(1, chips):
         left_copy(c, same_core(a), left_send.at[a]).wait_send()
         left_copy(same_core(a), sibling, left_fwd.at[a]).wait_send()
-    for dz in range(nr):
+    for block in range(nr):
         for t in range(ratio):
-            if dz:
-                right_copy(dz, t).wait_send()
-            else:
-                @pl.when(r * ratio + t != c)
-                def _(t=t):
-                    right_copy(0, t).wait_send()
+            @pl.when(block * ratio + t != c)
+            def _(block=block, t=t):
+                right_copy(block, t).wait_send()
+
+            @pl.when(jnp.logical_and(r >= block, r < nr - 1))
+            def _(block=block, t=t):
+                chain_copy(block, t, r + 1, up_send.at[block, t]).wait_send()
+
+            @pl.when(jnp.logical_and(r <= block, r > 0))
+            def _(block=block, t=t):
+                chain_copy(block, t, r - 1, down_send.at[block, t]).wait_send()
 
 
 def solution(mesh):
@@ -190,15 +238,18 @@
                 pltpu.VMEM((flat, width), BF16),
                 pltpu.VMEM((flat, width), F32),
                 pltpu.VMEM((nc, flat, width), BF16),
-                pltpu.VMEM((ratio, cols, cols, width), BF16),
+                pltpu.VMEM((nr, ratio, cols, cols, width), BF16),
                 pltpu.VMEM((nc, cols, cols, width), BF16),
                 pltpu.VMEM((rows, cols, width), F32),
                 pltpu.VMEM((rows, cols, width), F32),
                 dma((nc // 2,)),
                 dma((nc // 2,)),
                 dma((nc,)),
-                dma((nr * ratio,)),
+                dma((nr, ratio)),
                 dma((nc,)),
+                dma((nr, ratio)),
+                dma((nr, ratio)),
+                dma((nr, ratio)),
             ],
             compiler_params=pltpu.CompilerParams(collective_id=0, has_side_effects=True),
         )(

time: 26 us -> 26.1 us (level)
  the two profiles are of different devices: /device:TPU:12 before, /device:TPU:6 now
where the time goes in v2:
time: 26.1 us; the launch traced here: 25.9 us
  Pallas kernels  24.4 us (93%)
  local copies, waits for them, and re-layouts  1.57 us (6%)
    pallas_call x1, Pallas kernels, per_device(): pl.pallas_call(functools.partial(kernel, nr, nc), out_shape=jax.ShapeDtyp...  24.4 us
    unnamed x1, local copies, waits for them, and re-layouts  1.57 us

profile of v2, /device:TPU:6, one launch (start us, length us, event | category | flops | bytes accessed | tf_op | source)
XLA Modules:
  0.0 25.9 jit_solution(3648259021859224900)
XLA Ops:
  0.0 24.4 %shard_map.91 = bf16[32,16,128]{2,1,0:T(8,128)(2,1)} custom-call(bf16[32,16,128]{2,1,0:T(8,128)(2,1)} %pair.1, f32[1,128]{1,0:T(1,128)} %bitcast.2, bf16[128,128]{1,0:T(8,128)(2,1)} %w_left_gate.1, bf16[128,128]{1,0:T(8,128)(2,1)} %w_left.1, bf16[128,128]{1,0:T(8,128)(2,1)} %w_right_gate.1, bf16[128,128]{1,0:T(8,128)(2,1)} %w_right.1, f32[1,128]{1,0:T(1,128)} %bitcast.3, ...), custom_call_target="tpu_custom_call" | custom-call | tf_op jit(solution)/shard_map/pallas_call | solution.py:231
  24.4 1.6 %copy.11 = bf16[32,16,128]{2,1,0:T(8,128)(2,1)} copy(bf16[32,16,128]{2,1,0:T(8,128)(2,1)} %shard_map.91) | data formatting | bytes 262144

commit v3 on v2

v3 whole, which is shorter than its diff:
```python
import functools

import jax
import jax.numpy as jnp
from jax import lax
from jax.experimental import pallas as pl
from jax.experimental.pallas import tpu as pltpu
from jax.sharding import PartitionSpec as P

MESH = pl.DeviceIdType.MESH
F32 = jnp.float32
BF16 = jnp.bfloat16
GROUP = 8
PIECES = 1


def layer_norm(values, gain):
    mean = jnp.mean(values, axis=-1, keepdims=True)
    centred = values - mean
    variance = jnp.mean(centred * centred, axis=-1, keepdims=True)
    return centred * lax.rsqrt(variance + 1e-05) * gain


def gated(normed, w_gate, w):
    gate = jnp.dot(normed, w_gate, preferred_element_type=F32)
    value = jnp.dot(normed, w, preferred_element_type=F32)
    return (jax.nn.sigmoid(gate) * value).astype(BF16)


def kernel(
    nr, nc,
    pair, gain_in, w_left_gate, w_left, w_right_gate, w_right, gain_out, w_out_gate, w_out,
    out,
    normed_f, normed_t, gate, left_buf, chain, right_buf, left_f, acc,
    left_send, left_fwd, left_recv, right_send, right_recv, up_send, down_send, chain_recv,
):
    rows, cols, width = pair.shape
    ratio = nc // nr
    chips = nc // 2
    r = lax.axis_index("row")
    c = lax.axis_index("col")
    chip, core = c // 2, c % 2
    depth = cols // PIECES
    parts = [(t, u) for u in range(PIECES) for t in range(ratio)]
    sibling = chip * 2 + 1 - core

    def same_core(a):
        return (chip + a) % chips * 2 + core

    def other_core(a):
        return (chip + a) % chips * 2 + 1 - core

    barrier = pltpu.get_barrier_semaphore()

    def greet(row, col):
        pl.semaphore_signal(barrier, inc=1, device_id={"row": row, "col": col}, device_id_type=MESH)

    for s in range(1, nc):
        greet(r, (c + s) % nc)

    @pl.when(r > 0)
    def _():
        greet(r - 1, c)

    @pl.when(r < nr - 1)
    def _():
        greet(r + 1, c)

    def chain_copy(block, t, u, row, sem):
        piece = chain.at[block, t, pl.ds(u * depth, depth)]
        return pltpu.make_async_remote_copy(
            src_ref=piece, dst_ref=piece, send_sem=sem.at[block, t, u],
            recv_sem=chain_recv.at[block, t, u],
            device_id={"row": row, "col": c}, device_id_type=MESH,
        )

    def right_copy(block, t, u):
        return pltpu.make_async_remote_copy(
            src_ref=chain.at[block, t, pl.ds(u * depth, depth)],
            dst_ref=right_buf.at[c, pl.ds(u * depth, depth)],
            send_sem=right_send.at[block, t, u], recv_sem=right_recv.at[c, u],
            device_id={"row": r, "col": block * ratio + t}, device_id_type=MESH,
        )

    def left_copy(block, col, sem):
        return pltpu.make_async_remote_copy(
            src_ref=left_buf.at[block], dst_ref=left_buf.at[block],
            send_sem=sem, recv_sem=left_recv.at[block],
            device_id={"row": r, "col": col}, device_id_type=MESH,
        )

    def deliver(block, t, u):
        here = block * ratio + t == c

        @pl.when(here)
        def _():
            pltpu.make_async_copy(
                chain.at[block, t, pl.ds(u * depth, depth)],
                right_buf.at[c, pl.ds(u * depth, depth)],
                right_recv.at[c, u],
            ).start()

        @pl.when(jnp.logical_not(here))
        def _():
            right_copy(block, t, u).start()

    normed = layer_norm(pair[...].reshape(rows * cols, width).astype(F32), gain_in[...])
    normed_f[...] = normed
    for t, u in parts:
        for k in range(cols):
            normed_t[pl.ds((t * cols + k) * cols, cols), :] = normed_f[
                pl.ds(t * cols * cols + k, cols, stride=cols), :
            ].astype(BF16)
        block = normed_t[pl.ds(t * cols * cols, cols * cols), :]
        right = gated(block, w_right_gate[...], w_right[...])
        chain[r, t] = right.reshape(cols, cols, width)
        if t == 0:
            pl.semaphore_wait(
                barrier, nc - 1 + (r > 0).astype(jnp.int32) + (r < nr - 1).astype(jnp.int32)
            )

        @pl.when(r < nr - 1)
        def _(t=t, u=u):
            chain_copy(r, t, u, r + 1, up_send).start()

        @pl.when(r > 0)
        def _(t=t, u=u):
            chain_copy(r, t, u, r - 1, down_send).start()

    normed = normed.astype(BF16)
    left_buf[c] = gated(normed, w_left_gate[...], w_left[...])
    for a in range(1, chips):
        left_copy(c, same_core(a), left_send.at[a]).start()
    left_copy(c, sibling, left_send.at[0]).start()

    for t, u in parts:
        deliver(r, t, u)
    gate[...] = jax.nn.sigmoid(jnp.dot(normed, w_out_gate[...], preferred_element_type=F32))
    acc[...] = jnp.zeros_like(acc)

    def widen(block):
        left_f[block] = left_buf[block].astype(F32).reshape(rows, cols, width)

    widen(c)

    def relay(d):
        for t, u in parts:
            @pl.when(r - d >= 0)
            def _(t=t, u=u):
                block = r - d
                chain_copy(block, t, u, r, up_send).wait_recv()

                @pl.when(r < nr - 1)
                def _():
                    chain_copy(block, t, u, r + 1, up_send).start()

                deliver(block, t, u)

            @pl.when(r + d < nr)
            def _(t=t, u=u):
                block = r + d
                chain_copy(block, t, u, r, down_send).wait_recv()

                @pl.when(r > 0)
                def _():
                    chain_copy(block, t, u, r - 1, down_send).start()

                deliver(block, t, u)

    for d in range(1, nr - 1):
        relay(d)
    for a in range(1, chips):
        block = same_core(a)
        left_copy(block, sibling, left_fwd.at[a]).wait_recv()
        left_copy(block, sibling, left_fwd.at[a]).start()
        widen(block)
    relay(nr - 1)
    for a in range(chips):
        block = other_core(a)
        left_copy(block, sibling, left_send.at[0]).wait_recv()
        widen(block)

    def mix(block, u):
        pltpu.make_async_remote_copy(
            src_ref=chain.at[0, 0, pl.ds(0, depth)],
            dst_ref=right_buf.at[block, pl.ds(u * depth, depth)],
            send_sem=right_send.at[0, 0, 0], recv_sem=right_recv.at[block, u],
            device_id={"row": r, "col": sibling}, device_id_type=MESH,
        ).wait_recv()

        def group(g, carry):
            sums = [acc[g * GROUP + n] for n in range(GROUP)]
            for k in range(u * depth, (u + 1) * depth):
                other = right_buf[block, k].astype(F32)
                for n in range(GROUP):
                    sums[n] = sums[n] + left_f[block, g * GROUP + n, pl.ds(k, 1), :] * other
            for n in range(GROUP):
                acc[g * GROUP + n] = sums[n]
            return carry

        lax.fori_loop(0, rows // GROUP, group, 0)

    for u in range(PIECES):
        def step(s, carry, u=u):
            mix((chip + s // 2) % chips * 2 + (core + s) % 2, u)
            return carry

        lax.fori_loop(0, nc, step, 0)

    mixed = acc[...].reshape(rows * cols, width)
    out_normed = layer_norm(mixed, gain_out[...]).astype(BF16)
    update = gate[...] * jnp.dot(out_normed, w_out[...], preferred_element_type=F32)
    out[...] = update.astype(BF16).reshape(rows, cols, width)

    left_copy(c, sibling, left_send.at[0]).wait_send()
    for a in range(1, chips):
        left_copy(c, same_core(a), left_send.at[a]).wait_send()
        left_copy(same_core(a), sibling, left_fwd.at[a]).wait_send()
    for block in range(nr):
        for t, u in parts:
            @pl.when(block * ratio + t != c)
            def _(block=block, t=t, u=u):
                right_copy(block, t, u).wait_send()

            @pl.when(jnp.logical_and(r >= block, r < nr - 1))
            def _(block=block, t=t, u=u):
                chain_copy(block, t, u, r + 1, up_send).wait_send()

            @pl.when(jnp.logical_and(r <= block, r > 0))
            def _(block=block, t=t, u=u):
                chain_copy(block, t, u, r - 1, down_send).wait_send()


def solution(mesh):
    nr, nc = mesh.shape["row"], mesh.shape["col"]

    def per_device(
        pair, gain_in, w_left_gate, w_left, w_right_gate, w_right, gain_out, w_out_gate, w_out
    ):
        rows, cols, width = pair.shape
        flat = rows * cols
        ratio = nc // nr
        dma = pltpu.SemaphoreType.DMA
        return pl.pallas_call(
            functools.partial(kernel, nr, nc),
            out_shape=jax.ShapeDtypeStruct(pair.shape, BF16),
            in_specs=[pl.BlockSpec(memory_space=pltpu.VMEM)] * 9,
            out_specs=pl.BlockSpec(memory_space=pltpu.VMEM),
            scratch_shapes=[
                pltpu.VMEM((flat, width), F32),
                pltpu.VMEM((flat, width), BF16),
                pltpu.VMEM((flat, width), F32),
                pltpu.VMEM((nc, flat, width), BF16),
                pltpu.VMEM((nr, ratio, cols, cols, width), BF16),
                pltpu.VMEM((nc, cols, cols, width), BF16),
                pltpu.VMEM((nc, rows, cols, width), F32),
                pltpu.VMEM((rows, cols, width), F32),
                dma((nc // 2,)),
                dma((nc // 2,)),
                dma((nc,)),
                dma((nr, ratio, PIECES)),
                dma((nc, PIECES)),
                dma((nr, ratio, PIECES)),
                dma((nr, ratio, PIECES)),
                dma((nr, ratio, PIECES)),
            ],
            compiler_params=pltpu.CompilerParams(collective_id=0, has_side_effects=True),
        )(
            pair, gain_in.reshape(1, -1), w_left_gate, w_left, w_right_gate, w_right,
            gain_out.reshape(1, -1), w_out_gate, w_out,
        )

    return jax.shard_map(
        per_device,
        mesh=mesh,
        in_specs=(P("row", "col", None), P(), P(), P(), P(), P(), P(), P(), P()),
        out_specs=P("row", "col", None),
        check_vma=False,
    )
```

time: 26.1 us -> 24.4 us (0.935)
  the two profiles are of different devices: /device:TPU:6 before, /device:TPU:0 now
where the time goes in v3:
time: 24.4 us; the launch traced here: 24.1 us
  Pallas kernels  22.5 us (92%)
  local copies, waits for them, and re-layouts  1.57 us (6%)
    pallas_call x1, Pallas kernels, per_device(): pl.pallas_call(functools.partial(kernel, nr, nc), out_shape=jax.ShapeDtyp...  22.5 us
    unnamed x1, local copies, waits for them, and re-layouts  1.57 us

profile of v3, /device:TPU:0, one launch (start us, length us, event | category | flops | bytes accessed | tf_op | source)
XLA Modules:
  0.0 24.1 jit_solution(15449386395694099123)
XLA Ops:
  0.0 22.5 %shard_map.91 = bf16[32,16,128]{2,1,0:T(8,128)(2,1)} custom-call(bf16[32,16,128]{2,1,0:T(8,128)(2,1)} %pair.1, f32[1,128]{1,0:T(1,128)} %bitcast.2, bf16[128,128]{1,0:T(8,128)(2,1)} %w_left_gate.1, bf16[128,128]{1,0:T(8,128)(2,1)} %w_left.1, bf16[128,128]{1,0:T(8,128)(2,1)} %w_right_gate.1, bf16[128,128]{1,0:T(8,128)(2,1)} %w_right.1, f32[1,128]{1,0:T(1,128)} %bitcast.3, ...), custom_call_target="tpu_custom_call" | custom-call | tf_op jit(solution)/shard_map/pallas_call | solution.py:244
  22.5 1.6 %copy.11 = bf16[32,16,128]{2,1,0:T(8,128)(2,1)} copy(bf16[32,16,128]{2,1,0:T(8,128)(2,1)} %shard_map.91) | data formatting | bytes 262144

commit v4 on v3

--- a/solution.py
+++ b/solution.py
@@ -10,7 +10,7 @@
 MESH = pl.DeviceIdType.MESH
 F32 = jnp.float32
 BF16 = jnp.bfloat16
-GROUP = 8
+GROUP = 16
 PIECES = 1
 
 

time: 24.4 us -> 24.3 us (level)
  no operation moved by 1% of the time
where the time goes in v4:
time: 24.3 us; the launch traced here: 23.9 us
  Pallas kernels  22.3 us (92%)
  local copies, waits for them, and re-layouts  1.57 us (6%)
    pallas_call x1, Pallas kernels, per_device(): pl.pallas_call(functools.partial(kernel, nr, nc), out_shape=jax.ShapeDtyp...  22.3 us
    unnamed x1, local copies, waits for them, and re-layouts  1.57 us

profile of v4, /device:TPU:0, one launch (start us, length us, event | category | flops | bytes accessed | tf_op | source)
XLA Modules:
  0.0 23.9 jit_solution(4930850302397276997)
XLA Ops:
  0.0 22.3 %shard_map.91 = bf16[32,16,128]{2,1,0:T(8,128)(2,1)} custom-call(bf16[32,16,128]{2,1,0:T(8,128)(2,1)} %pair.1, f32[1,128]{1,0:T(1,128)} %bitcast.2, bf16[128,128]{1,0:T(8,128)(2,1)} %w_left_gate.1, bf16[128,128]{1,0:T(8,128)(2,1)} %w_left.1, bf16[128,128]{1,0:T(8,128)(2,1)} %w_right_gate.1, bf16[128,128]{1,0:T(8,128)(2,1)} %w_right.1, f32[1,128]{1,0:T(1,128)} %bitcast.3, ...), custom_call_target="tpu_custom_call" | custom-call | tf_op jit(solution)/shard_map/pallas_call | solution.py:244
  22.3 1.6 %copy.11 = bf16[32,16,128]{2,1,0:T(8,128)(2,1)} copy(bf16[32,16,128]{2,1,0:T(8,128)(2,1)} %shard_map.91) | data formatting | bytes 262144
